TPU v7x, 32 devices: a whole 2x2x4 slice. The times are simulated.
32 devices in a mesh: sec: 4 (over y, x), dom: 8 (over z, core).
Axes of the slice: x: 2, y: 2, z: 4, core: 2. Of those that a mesh axis runs over, the one named last changes fastest.
Arguments:
- disp_coarse: float32 [4096], P('dom'), may hold values from -6 to 6
- support_ids: int32 [4, 8, 4], P('sec', 'dom'), may hold values from 0 to 7, all different within a row
- rbf_weights: bfloat16 [4, 8, 4, 512, 64], P('sec', 'dom'), may hold values from -0.125 to 0.125
- flow: float32 [4, 4, 512, 256], P('sec', None, 'dom'), may hold values from -6 to 6
- pivots: int32 [4096], replicated, may hold values from 0 to 4095, each once
- lower_inverse: float32 [4096, 4096], P('dom'), as said below
- upper_inverse: float32 [4096, 4096], P('dom'), as said below
Outputs:
- new_flow: float32 [4, 4, 512, 256], P('sec', None, 'dom')
- new_disp: float32 [4096], P('dom')
Inputs may be any that keep to these rules, and one draw needn't show every extreme that they name: `support_ids`: each row names 4 different structure blocks; every block is named by some row. `pivots`: each index once. `lower_inverse`: unit lower triangular. `upper_inverse`: upper triangular with a positive diagonal.
All inputs are finite; a program needn't handle non-finite values.
Results may differ from a plain program's by a relative error of at most 0.00035.
Values may be sent and summed in bfloat16 or wider, within the bound.
No kernel may reach another device: no remote copies, remote signals or barrier semaphores. Data moves between devices by JAX's collectives and lax.ppermute only.
A program may use at most 64 MiB of HBM per device.

v0:
```python
import jax
import jax.numpy as jnp
from jax import lax
from jax.sharding import PartitionSpec as P

ITERS = 4
COURANT = 0.4
MACH = 0.5
DISSIPATION = 0.03125
FACE_AREA = 0.125


def padded_2(cells, sides, width):
    for axis, dim in sides:
        count = lax.axis_size(axis)
        head = lax.slice_in_dim(cells, 0, width, axis=dim)
        tail = lax.slice_in_dim(cells, cells.shape[dim] - width, cells.shape[dim], axis=dim)
        cells = jnp.concatenate(
            [
                lax.ppermute(tail, axis, [(i, (i + 1) % count) for i in range(count)]),
                cells,
                lax.ppermute(head, axis, [((i + 1) % count, i) for i in range(count)]),
            ],
            axis=dim,
        )
    return cells


def stencil(padded):
    z_extent = padded.shape[1]
    y_extent = padded.shape[2]
    y_padded = jnp.pad(padded, ((0, 0), (0, 0), (2, 2)))

    def zshift(offset):
        return y_padded[:, 2 + offset : z_extent - 2 + offset, 2 : y_extent + 2]

    def yshift(offset):
        return y_padded[:, 2 : z_extent - 2, 2 + offset : y_extent + 2 + offset]

    centre = zshift(0)
    z_slope = 0.5 * (zshift(1) - zshift(-1))
    y_slope = 0.5 * (yshift(1) - yshift(-1))
    z_fourth = zshift(2) - 4.0 * zshift(1) + 6.0 * centre - 4.0 * zshift(-1) + zshift(-2)
    y_fourth = yshift(2) - 4.0 * yshift(1) + 6.0 * centre - 4.0 * yshift(-1) + yshift(-2)
    damping = DISSIPATION * (z_fourth + y_fourth)
    density = centre[0] - COURANT * (MACH * z_slope[0] + z_slope[2] + y_slope[3]) - damping[0]
    pressure = centre[1] - COURANT * (MACH * z_slope[1] + z_slope[2] + y_slope[3]) - damping[1]
    along = centre[2] - COURANT * (MACH * z_slope[2] + z_slope[1]) - damping[2]
    normal = centre[3] - COURANT * (MACH * z_slope[3] + y_slope[1]) - damping[3]
    return jnp.stack([density, pressure, along, normal])


def with_rims(fields):
    return padded_2(fields, (("dom", 1),), 2)


def shards(disp_coarse, support_ids, rbf_weights, flow, pivots, lower_inverse, upper_inverse):
    block_size = disp_coarse.shape[0]
    domains = lax.axis_size("dom")
    coarse_table = lax.all_gather(
        disp_coarse.astype(jnp.bfloat16), "dom", axis=0, tiled=True
    ).reshape(domains, block_size)
    support = support_ids[0, 0]
    weights = rbf_weights[0, 0]
    matches = support[:, None] == lax.broadcasted_iota(jnp.int32, (support.shape[0], domains), 1)
    choose = matches.astype(jnp.bfloat16)
    picked = jnp.dot(choose, coarse_table, preferred_element_type=jnp.float32).astype(jnp.bfloat16)
    wall_motion = jnp.einsum("kj,kjz->z", picked, weights, preferred_element_type=jnp.float32)
    fields = flow[0].at[3, :, 0].set(wall_motion)
    for sweep_index in range(ITERS):
        fields = stencil(with_rims(fields))
    push = (FACE_AREA * fields[1, :, 0]).astype(jnp.bfloat16)
    terms = jnp.einsum("kjz,z->kj", weights, push, preferred_element_type=jnp.float32)
    dense = jnp.einsum(
        "kb,kj->bj", matches.astype(jnp.float32), terms, precision=lax.Precision.HIGHEST
    )
    owned = lax.psum_scatter(dense, "dom", scatter_dimension=0, tiled=True)
    owned = lax.psum(owned, "sec")
    forces = lax.all_gather(owned, "dom", axis=0, tiled=True).reshape(-1)
    permuted = jnp.take(forces, pivots, axis=0)
    lower_part = jnp.dot(lower_inverse, permuted, precision=lax.Precision.HIGHEST)
    middle = lax.all_gather(lower_part, "dom", axis=0, tiled=True)
    solved = jnp.dot(upper_inverse, middle, precision=lax.Precision.HIGHEST)
    new_disp = 0.5 * disp_coarse + 0.5 * solved
    return (fields[None], new_disp)


def solution(mesh):
    return jax.shard_map(
        shards,
        mesh=mesh,
        in_specs=(
            P("dom"),
            P("sec", "dom", None),
            P("sec", "dom", None, None, None),
            P("sec", None, "dom", None),
            P(),
            P("dom", None),
            P("dom", None),
        ),
        out_specs=(P("sec", None, "dom", None), P("dom")),
        check_vma=False,
    )
```

profile of v0, /device:TPU:0, one launch (start us, length us, event | category | flops | bytes accessed | tf_op | source)
XLA Modules:
  0.0 148.1 jit_solution(1845433395327403583)
XLA Ops:
  0.6 0.0 copy-start
  0.6 1.0 copy.27
  1.6 0.7 convert_element_type.19
  2.3 14.5 %all-gather = bf16[8,1,512]{2,1,0:T(2,128)(2,1)S(1)} all-gather(bf16[1,1,512]{2,1,0:T(2,128)(2,1)S(1)} %reshape.142), channel_id=1, replica_groups=mesh['sec'=4,'dom'=8] {'dom'}, dimensions={0}, use_global_device_ids=true | all-gather | bytes 9216 | tf_op jit(solution)/shard_map/all_gather | solution.py:60
  16.8 0.8 fusion
  17.6 0.0 copy-done
  17.6 0.2 convolution_bitcast_fusion
  17.8 0.2 scatter.4
  18.0 2.1 %collective-permute-start = (f32[4,2,256]{2,1,0:T(2,128)S(1)}, f32[4,2,256]{2,1,0:T(2,128)S(1)}, u32[]{:S(2)}, u32[]{:S(2)}) collective-permute-start(f32[4,2,256]{2,1,0:T(2,128)S(1)} %get-tuple-element.55), channel_id=1, source_target_pairs={{1,0},{2,1},{3,2},{4,3},{5,4},{6,5},{7,6},{0,7},{9,8},{10,9},{11,1... | collective-permute-start | bytes 24584 | tf_op jit(solution)/shard_map/ppermute | solution.py:22
  20.1 0.0 collective-permute-start.1
  20.1 1.4 collective-permute-done
  21.5 3.5 %collective-permute-done.1 = f32[4,2,256]{2,1,0:T(2,128)S(1)} collective-permute-done((f32[4,2,256]{2,1,0:T(2,128)S(1)}, f32[4,2,256]{2,1,0:T(2,128)S(1)}, u32[]{:S(2)}, u32[]{:S(2)}) %collective-permute-start.1) | collective-permute-done | bytes 8224 | tf_op jit(solution)/shard_map/ppermute | solution.py:20
  25.0 0.2 select_maximum_fusion.15
  25.2 0.0 copy-start.1
  25.2 0.0 copy-start.4
  25.2 0.4 subtract_multiply_fusion.6
  25.6 0.1 slice_subtract_fusion.24
  25.7 0.1 collective-permute-start.2
  25.8 0.5 collective-permute-start.3
  26.3 0.9 collective-permute-done.2
  27.2 3.6 %collective-permute-done.3 = f32[4,2,256]{2,1,0:T(2,128)S(1)} collective-permute-done((f32[4,2,256]{2,1,0:T(2,128)S(1)}, f32[4,2,256]{2,1,0:T(2,128)S(1)}, u32[]{:S(2)}, u32[]{:S(2)}) %collective-permute-start.3) | collective-permute-done | bytes 8224 | tf_op jit(solution)/shard_map/ppermute | solution.py:20
  30.7 0.2 select_maximum_fusion.10
  31.0 0.0 copy-start.3
  31.0 0.3 subtract_multiply_fusion.5
  31.4 0.1 slice_subtract_fusion.18
  31.5 0.1 collective-permute-start.4
  31.5 0.5 collective-permute-start.5
  32.0 0.9 collective-permute-done.4
  32.9 3.6 %collective-permute-done.5 = f32[4,2,256]{2,1,0:T(2,128)S(1)} collective-permute-done((f32[4,2,256]{2,1,0:T(2,128)S(1)}, f32[4,2,256]{2,1,0:T(2,128)S(1)}, u32[]{:S(2)}, u32[]{:S(2)}) %collective-permute-start.5) | collective-permute-done | bytes 8224 | tf_op jit(solution)/shard_map/ppermute | solution.py:20
  36.5 0.2 select_maximum_fusion.5
  36.7 0.3 subtract_multiply_fusion.3
  37.1 0.1 slice_subtract_fusion.14
  37.2 0.1 collective-permute-start.6
  37.2 0.5 collective-permute-start.7
  37.7 0.0 copy-done.1
  37.8 0.0 copy-done.4
  37.8 0.6 dynamic-slice.10
  38.4 0.3 collective-permute-done.6
  38.6 3.6 %collective-permute-done.7 = f32[4,2,256]{2,1,0:T(2,128)S(1)} collective-permute-done((f32[4,2,256]{2,1,0:T(2,128)S(1)}, f32[4,2,256]{2,1,0:T(2,128)S(1)}, u32[]{:S(2)}, u32[]{:S(2)}) %collective-permute-start.7) | collective-permute-done | bytes 8224 | tf_op jit(solution)/shard_map/ppermute | solution.py:20
  42.2 0.2 select_maximum_fusion
  42.4 0.3 subtract_multiply_fusion.1
  42.8 0.1 slice_subtract_fusion.10
  42.8 0.1 fusion.58
  43.0 0.1 fusion.30
  43.1 0.0 copy-done.3
  43.1 0.3 fusion.62
  43.4 25.9 %all-reduce.4 = f32[8,512]{1,0:T(8,128)S(1)} all-reduce(f32[8,512]{1,0:T(8,128)S(1)} %fusion.62), channel_id=2, replica_groups=mesh['sec'=4,'dom'=8] {'dom'}, use_global_device_ids=true, to_apply=%region_0.0.clone | all-reduce | flops 4096 | bytes 32768
  69.3 0.6 constant_dynamic-slice_fusion
  69.9 9.9 %psum.7 = f32[1,512]{1,0:T(1,128)S(1)} all-reduce(f32[1,512]{1,0:T(1,128)S(1)} %constant_dynamic-slice_fusion), channel_id=1, replica_groups=mesh['sec'=4,'dom'=8] {'sec'}, use_global_device_ids=true, to_apply=%region_1.2 | all-reduce | flops 512 | bytes 4096 | tf_op jit(solution)/shard_map/psum | solution.py:78
  79.8 12.8 %all-gather.1 = f32[8,1,512]{2,1,0:T(1,128)S(1)} all-gather(f32[1,1,512]{2,1,0:T(1,128)S(1)} %bitcast.46), channel_id=1, replica_groups=mesh['sec'=4,'dom'=8] {'dom'}, dimensions={0}, use_global_device_ids=true | all-gather | bytes 18432 | tf_op jit(solution)/shard_map/all_gather | solution.py:79
  92.6 23.0 %gather_fusion = f32[4096]{0:T(1024)S(1)} fusion(f32[4096]{0:T(1024)S(1)} %bitcast.41, s32[4096]{0:T(1024)S(1)} %fusion.59), kind=kCustom, calls=%fused_computation | custom fusion | bytes 49152 | tf_op jit(solution)/shard_map/jit(_take)/gather | solution.py:80
  115.6 0.0 copy-start.2
  115.7 9.2 %convolution_bitcast_fusion.1 = f32[1,1,512]{2,1,0:T(1,128)S(1)} fusion(f32[4096,1]{0,1:T(1,128)S(1)} %bitcast.43, f32[512,4096]{1,0:T(8,128)} %param.14), kind=kOutput, calls=%fused_computation.4 | convolution fusion | flops 25165824 | bytes 8407040 | tf_op jit(solution)/shard_map/dot_general | solution.py:81
  124.8 12.8 %all-gather.2 = f32[8,1,512]{2,1,0:T(1,128)S(1)} all-gather(f32[1,1,512]{2,1,0:T(1,128)S(1)} %convolution_bitcast_fusion.1), channel_id=1, replica_groups=mesh['sec'=4,'dom'=8] {'dom'}, dimensions={0}, use_global_device_ids=true | all-gather | bytes 18432 | tf_op jit(solution)/shard_map/all_gather | solution.py:82
  137.6 9.2 %fusion.73 = f32[1,512]{1,0:T(1,128)S(1)} fusion(f32[4096,1]{0,1:T(1,128)S(1)} %bitcast.44, f32[512,4096]{1,0:T(8,128)} %param.15), kind=kOutput, calls=%fused_computation.170 | convolution fusion | flops 25165824 | bytes 8407040 | tf_op jit(solution)/shard_map/dot_general | solution.py:83
  146.8 0.0 copy-done.2
  146.8 0.6 add_multiply_fusion
  147.4 0.7 maximum_bitcast_fusion
  (13 shorter events, 0.2 us)
Async XLA Ops:
  0.6 17.0 %copy-start = (bf16[1,1,4,512,64]{3,4,2,1,0:T(8,128)(2,1)S(1)}, bf16[1,1,4,512,64]{3,4,2,1,0:T(8,128)(2,1)}, u32[]{:S(2)}) copy-start(bf16[1,1,4,512,64]{3,4,2,1,0:T(8,128)(2,1)} %param.11) | copy-start | bytes 786436
  18.0 3.5 %collective-permute-start = (f32[4,2,256]{2,1,0:T(2,128)S(1)}, f32[4,2,256]{2,1,0:T(2,128)S(1)}, u32[]{:S(2)}, u32[]{:S(2)}) collective-permute-start(f32[4,2,256]{2,1,0:T(2,128)S(1)} %get-tuple-element.55), channel_id=1, source_target_pairs={{1,0},{2,1},{3,2},{4,3},{5,4},{6,5},{7,6},{0,7},{9,8},{10,9},{11,1... | collective-permute-start | bytes 24584 | tf_op jit(solution)/shard_map/ppermute | solution.py:22
  20.1 4.9 %collective-permute-start.1 = (f32[4,2,256]{2,1,0:T(2,128)S(1)}, f32[4,2,256]{2,1,0:T(2,128)S(1)}, u32[]{:S(2)}, u32[]{:S(2)}) collective-permute-start(f32[4,2,256]{2,1,0:T(2,128)S(1)} %get-tuple-element.54), channel_id=1, source_target_pairs={{0,1},{1,2},{2,3},{3,4},{4,5},{5,6},{6,7},{7,0},{8,9},{9,10},{10,1... | collective-permute-start | bytes 24584 | tf_op jit(solution)/shard_map/ppermute | solution.py:20
  25.2 12.5 %copy-start.1 = (s32[4096]{0:T(1024)S(1)}, s32[4096]{0:T(1024)}, u32[]{:S(2)}) copy-start(s32[4096]{0:T(1024)} %param.13) | copy-start | bytes 49156
  25.2 12.5 %copy-start.4 = (u32[32]{0:T(128)S(1)}, u32[32]{0:T(128)}, u32[]{:S(2)}) copy-start(u32[32]{0:T(128)} %constant.79) | copy-start | bytes 388
  25.7 1.4 collective-permute-start.2
  25.8 4.9 %collective-permute-start.3 = (f32[4,2,256]{2,1,0:T(2,128)S(1)}, f32[4,2,256]{2,1,0:T(2,128)S(1)}, u32[]{:S(2)}, u32[]{:S(2)}) collective-permute-start(f32[4,2,256]{2,1,0:T(2,128)S(1)} %get-tuple-element.52), channel_id=1, source_target_pairs={{0,1},{1,2},{2,3},{3,4},{4,5},{5,6},{6,7},{7,0},{8,9},{9,10},{10,1... | collective-permute-start | bytes 24584 | tf_op jit(solution)/shard_map/ppermute | solution.py:20
  31.0 12.1 %copy-start.3 = (s32[1,1,4]{2,1,0:T(1,128)S(1)}, s32[1,1,4]{2,1,0:T(1,128)}, u32[]{:S(2)}) copy-start(s32[1,1,4]{2,1,0:T(1,128)} %param.10) | copy-start | bytes 52
  31.5 1.4 collective-permute-start.4
  31.5 4.9 %collective-permute-start.5 = (f32[4,2,256]{2,1,0:T(2,128)S(1)}, f32[4,2,256]{2,1,0:T(2,128)S(1)}, u32[]{:S(2)}, u32[]{:S(2)}) collective-permute-start(f32[4,2,256]{2,1,0:T(2,128)S(1)} %get-tuple-element.48), channel_id=1, source_target_pairs={{0,1},{1,2},{2,3},{3,4},{4,5},{5,6},{6,7},{7,0},{8,9},{9,10},{10,1... | collective-permute-start | bytes 24584 | tf_op jit(solution)/shard_map/ppermute | solution.py:20
  37.2 1.4 collective-permute-start.6
  37.2 4.9 %collective-permute-start.7 = (f32[4,2,256]{2,1,0:T(2,128)S(1)}, f32[4,2,256]{2,1,0:T(2,128)S(1)}, u32[]{:S(2)}, u32[]{:S(2)}) collective-permute-start(f32[4,2,256]{2,1,0:T(2,128)S(1)} %get-tuple-element.44), channel_id=1, source_target_pairs={{0,1},{1,2},{2,3},{3,4},{4,5},{5,6},{6,7},{7,0},{8,9},{9,10},{10,1... | collective-permute-start | bytes 24584 | tf_op jit(solution)/shard_map/ppermute | solution.py:20
  115.6 31.2 %copy-start.2 = (f32[512]{0:T(512)S(1)}, f32[512]{0:T(512)}, u32[]{:S(2)}) copy-start(f32[512]{0:T(512)} %param.9) | copy-start | bytes 6148
where the time goes:
time: 148 us
  blocking collectives  75.8 us (51%)
  local copies, waits for them, and re-layouts  25.5 us (17%)
  matrix products  19.8 us (13%)
  waiting for transfers between devices  17.5 us (12%)
  other arithmetic  4.78 us (3%)
  starting transfers between devices  3.77 us (3%)
    unnamed x1, blocking collectives  25.9 us
    gather x1, local copies, waits for them, and re-layouts, shards(): permuted = jnp.take(forces, pivots, axis=0)  23 us
    all_gather x1, blocking collectives, shards(): lax.all_gather(disp_coarse.astype(jnp.bfloat16), 'dom', axis=0, tiled=True)  14.5 us
    ppermute x4, waiting for transfers between devices, padded_2(): lax.ppermute(tail, axis, [(i, (i + 1) % count) for i in range(count)])  14.2 us
    all_gather x1, blocking collectives, shards(): middle = lax.all_gather(lower_part, 'dom', axis=0, tiled=True)  12.8 us
    all_gather x1, blocking collectives, shards(): forces = lax.all_gather(owned, 'dom', axis=0, tiled=True).reshape(-1)  12.8 us
    psum x1, blocking collectives, shards(): owned = lax.psum(owned, 'sec')  9.91 us
    dot_general x1, matrix products, shards(): jnp.dot(lower_inverse, permuted, precision=lax.Precision.HIGHEST)  9.19 us
  transfers between devices with their start and end apart: 8, of which 8 were waited for; matrix products, arithmetic and copies ran while one was open for 0% of the time, Pallas kernels for 0%

commit v1 on v0

--- a/solution.py
+++ b/solution.py
@@ -79,7 +79,12 @@
     forces = lax.all_gather(owned, "dom", axis=0, tiled=True).reshape(-1)
     permuted = jnp.take(forces, pivots, axis=0)
     lower_part = jnp.dot(lower_inverse, permuted, precision=lax.Precision.HIGHEST)
-    middle = lax.all_gather(lower_part, "dom", axis=0, tiled=True)
+    ring = [lower_part]
+    for hop in range(7):
+        ring.append(lax.ppermute(ring[-1], "dom", [(dev, (dev + 1) % 8) for dev in range(8)]))
+    middle = jnp.roll(
+        jnp.concatenate(ring[::-1], axis=0), (lax.axis_index("dom") + 1) * ring[0].shape[0], axis=0
+    )
     solved = jnp.dot(upper_inverse, middle, precision=lax.Precision.HIGHEST)
     new_disp = 0.5 * disp_coarse + 0.5 * solved
     return (fields[None], new_disp)

time: 148 us -> 169 us (1.14)
  waiting for transfers between devices: 17.5 us -> 50.1 us
  blocking collectives: 75.8 us -> 63 us
    ppermute x0 -> x7, waiting for transfers between devices: none -> 32.6 us  [shards(): lax.ppermute(ring[-1], 'dom', [(dev, (dev + 1) % 8) for dev in range(8)])]
    all_gather x1 -> x0, blocking collectives: 12.8 us -> none  [shards(): middle = lax.all_gather(lower_part, 'dom', axis=0, tiled=True)]
  transfers between devices with their start and end apart: 8 -> 15, of which waited for: 8 -> 15; matrix products, arithmetic and copies ran while one was open for 0% -> 1% of each run, Pallas kernels for 0% -> 0%
where the time goes in v1:
time: 169 us
  blocking collectives  63 us (37%)
  waiting for transfers between devices  50.1 us (30%)
  local copies, waits for them, and re-layouts  25.7 us (15%)
  matrix products  19.8 us (12%)
  other arithmetic  4.78 us (3%)
  starting transfers between devices  4.13 us (2%)
    ppermute x7, waiting for transfers between devices, shards(): lax.ppermute(ring[-1], 'dom', [(dev, (dev + 1) % 8) for dev in range(8)])  32.6 us
    unnamed x1, blocking collectives  25.9 us
    gather x1, local copies, waits for them, and re-layouts, shards(): permuted = jnp.take(forces, pivots, axis=0)  23 us
    all_gather x1, blocking collectives, shards(): lax.all_gather(disp_coarse.astype(jnp.bfloat16), 'dom', axis=0, tiled=True)  14.5 us
    ppermute x4, waiting for transfers between devices, padded_2(): lax.ppermute(tail, axis, [(i, (i + 1) % count) for i in range(count)])  14.2 us
    all_gather x1, blocking collectives, shards(): forces = lax.all_gather(owned, 'dom', axis=0, tiled=True).reshape(-1)  12.8 us
    psum x1, blocking collectives, shards(): owned = lax.psum(owned, 'sec')  9.92 us
    dot_general x1, matrix products, shards(): jnp.dot(lower_inverse, permuted, precision=lax.Precision.HIGHEST)  9.19 us
  transfers between devices with their start and end apart: 15, of which 15 were waited for; matrix products, arithmetic and copies ran while one was open for 1% of the time, Pallas kernels for 0%

profile of v1, /device:TPU:0, one launch (start us, length us, event | category | flops | bytes accessed | tf_op | source)
XLA Modules:
  0.0 168.6 jit_solution(14471032041497977545)
XLA Ops:
  0.6 0.0 copy-start
  0.6 1.0 copy.43
  1.6 0.7 convert_element_type.19
  2.3 14.5 %all-gather = bf16[8,1,512]{2,1,0:T(2,128)(2,1)S(1)} all-gather(bf16[1,1,512]{2,1,0:T(2,128)(2,1)S(1)} %reshape.142), channel_id=1, replica_groups=mesh['sec'=4,'dom'=8] {'dom'}, dimensions={0}, use_global_device_ids=true | all-gather | bytes 9216 | tf_op jit(solution)/shard_map/all_gather | solution.py:60
  16.8 0.8 fusion
  17.6 0.2 convolution_bitcast_fusion
  17.8 0.2 scatter.4
  18.0 2.1 %collective-permute-start = (f32[4,2,256]{2,1,0:T(2,128)S(1)}, f32[4,2,256]{2,1,0:T(2,128)S(1)}, u32[]{:S(2)}, u32[]{:S(2)}) collective-permute-start(f32[4,2,256]{2,1,0:T(2,128)S(1)} %get-tuple-element.55), channel_id=1, source_target_pairs={{1,0},{2,1},{3,2},{4,3},{5,4},{6,5},{7,6},{0,7},{9,8},{10,9},{11,1... | collective-permute-start | bytes 24584 | tf_op jit(solution)/shard_map/ppermute | solution.py:22
  20.1 0.0 collective-permute-start.1
  20.1 1.4 collective-permute-done
  21.5 3.5 %collective-permute-done.1 = f32[4,2,256]{2,1,0:T(2,128)S(1)} collective-permute-done((f32[4,2,256]{2,1,0:T(2,128)S(1)}, f32[4,2,256]{2,1,0:T(2,128)S(1)}, u32[]{:S(2)}, u32[]{:S(2)}) %collective-permute-start.1) | collective-permute-done | bytes 8224 | tf_op jit(solution)/shard_map/ppermute | solution.py:20
  25.0 0.2 select_maximum_fusion.15
  25.2 0.0 copy-start.1
  25.2 0.0 copy-start.4
  25.2 0.4 subtract_multiply_fusion.6
  25.6 0.1 slice_subtract_fusion.24
  25.7 0.1 collective-permute-start.2
  25.8 0.5 collective-permute-start.3
  26.3 0.9 collective-permute-done.2
  27.2 3.6 %collective-permute-done.3 = f32[4,2,256]{2,1,0:T(2,128)S(1)} collective-permute-done((f32[4,2,256]{2,1,0:T(2,128)S(1)}, f32[4,2,256]{2,1,0:T(2,128)S(1)}, u32[]{:S(2)}, u32[]{:S(2)}) %collective-permute-start.3) | collective-permute-done | bytes 8224 | tf_op jit(solution)/shard_map/ppermute | solution.py:20
  30.7 0.2 select_maximum_fusion.10
  31.0 0.0 copy-start.3
  31.0 0.3 subtract_multiply_fusion.5
  31.3 0.1 slice_subtract_fusion.18
  31.5 0.1 collective-permute-start.4
  31.5 0.5 collective-permute-start.5
  32.0 0.9 collective-permute-done.4
  32.9 3.6 %collective-permute-done.5 = f32[4,2,256]{2,1,0:T(2,128)S(1)} collective-permute-done((f32[4,2,256]{2,1,0:T(2,128)S(1)}, f32[4,2,256]{2,1,0:T(2,128)S(1)}, u32[]{:S(2)}, u32[]{:S(2)}) %collective-permute-start.5) | collective-permute-done | bytes 8224 | tf_op jit(solution)/shard_map/ppermute | solution.py:20
  36.5 0.2 select_maximum_fusion.5
  36.7 0.3 subtract_multiply_fusion.3
  37.1 0.1 slice_subtract_fusion.14
  37.2 0.1 collective-permute-start.6
  37.2 0.5 collective-permute-start.7
  37.8 0.6 dynamic-slice.10
  38.3 0.3 collective-permute-done.6
  38.6 3.6 %collective-permute-done.7 = f32[4,2,256]{2,1,0:T(2,128)S(1)} collective-permute-done((f32[4,2,256]{2,1,0:T(2,128)S(1)}, f32[4,2,256]{2,1,0:T(2,128)S(1)}, u32[]{:S(2)}, u32[]{:S(2)}) %collective-permute-start.7) | collective-permute-done | bytes 8224 | tf_op jit(solution)/shard_map/ppermute | solution.py:20
  42.2 0.2 select_maximum_fusion
  42.4 0.3 subtract_multiply_fusion.1
  42.8 0.1 slice_subtract_fusion.10
  42.8 0.1 fusion.58
  42.9 0.1 fusion.30
  43.1 0.3 fusion.62
  43.4 25.9 %all-reduce.4 = f32[8,512]{1,0:T(8,128)S(1)} all-reduce(f32[8,512]{1,0:T(8,128)S(1)} %fusion.62), channel_id=2, replica_groups=mesh['sec'=4,'dom'=8] {'dom'}, use_global_device_ids=true, to_apply=%region_0.0.clone | all-reduce | flops 4096 | bytes 32768
  69.3 0.6 constant_dynamic-slice_fusion
  69.9 9.9 %psum.7 = f32[1,512]{1,0:T(1,128)S(1)} all-reduce(f32[1,512]{1,0:T(1,128)S(1)} %constant_dynamic-slice_fusion), channel_id=1, replica_groups=mesh['sec'=4,'dom'=8] {'sec'}, use_global_device_ids=true, to_apply=%region_1.2 | all-reduce | flops 512 | bytes 4096 | tf_op jit(solution)/shard_map/psum | solution.py:78
  79.8 12.8 %all-gather.1 = f32[8,1,512]{2,1,0:T(1,128)S(1)} all-gather(f32[1,1,512]{2,1,0:T(1,128)S(1)} %bitcast.44), channel_id=1, replica_groups=mesh['sec'=4,'dom'=8] {'dom'}, dimensions={0}, use_global_device_ids=true | all-gather | bytes 18432 | tf_op jit(solution)/shard_map/all_gather | solution.py:79
  92.6 23.0 %gather_fusion = f32[4096]{0:T(1024)S(1)} fusion(f32[4096]{0:T(1024)S(1)} %bitcast.36, s32[4096]{0:T(1024)S(1)} %fusion.59), kind=kCustom, calls=%fused_computation | custom fusion | bytes 49152 | tf_op jit(solution)/shard_map/jit(_take)/gather | solution.py:80
  115.7 0.0 copy-start.2
  115.7 9.2 %fusion.73 = f32[1,512]{1,0:T(1,128)S(1)} fusion(f32[4096,1]{0,1:T(1,128)S(1)} %bitcast.38, f32[512,4096]{1,0:T(8,128)} %param.14), kind=kOutput, calls=%fused_computation.185 | convolution fusion | flops 25165824 | bytes 8407040 | tf_op jit(solution)/shard_map/dot_general | solution.py:81
  124.9 0.4 collective-permute-start.8
  125.2 4.5 %collective-permute-done.8 = f32[512]{0:T(512)S(1)} collective-permute-done((f32[512]{0:T(512)S(1)}, f32[512]{0:T(512)S(1)}, u32[]{:S(2)}, u32[]{:S(2)}) %collective-permute-start.8) | collective-permute-done | bytes 2080 | tf_op jit(solution)/shard_map/ppermute | solution.py:84
  129.7 0.0 collective-permute-start.9
  129.7 4.8 %collective-permute-done.9 = f32[512]{0:T(512)S(1)} collective-permute-done((f32[512]{0:T(512)S(1)}, f32[512]{0:T(512)S(1)}, u32[]{:S(2)}, u32[]{:S(2)}) %collective-permute-start.9) | collective-permute-done | bytes 2080 | tf_op jit(solution)/shard_map/ppermute | solution.py:84
  134.5 4.8 %collective-permute-done.10 = f32[512]{0:T(512)S(1)} collective-permute-done((f32[512]{0:T(512)S(1)}, f32[512]{0:T(512)S(1)}, u32[]{:S(2)}, u32[]{:S(2)}) %collective-permute-start.10) | collective-permute-done | bytes 2080 | tf_op jit(solution)/shard_map/ppermute | solution.py:84
  139.3 4.8 %collective-permute-done.11 = f32[512]{0:T(512)S(1)} collective-permute-done((f32[512]{0:T(512)S(1)}, f32[512]{0:T(512)S(1)}, u32[]{:S(2)}, u32[]{:S(2)}) %collective-permute-start.11) | collective-permute-done | bytes 2080 | tf_op jit(solution)/shard_map/ppermute | solution.py:84
  144.1 4.8 %collective-permute-done.12 = f32[512]{0:T(512)S(1)} collective-permute-done((f32[512]{0:T(512)S(1)}, f32[512]{0:T(512)S(1)}, u32[]{:S(2)}, u32[]{:S(2)}) %collective-permute-start.12) | collective-permute-done | bytes 2080 | tf_op jit(solution)/shard_map/ppermute | solution.py:84
  148.9 4.8 %collective-permute-done.13 = f32[512]{0:T(512)S(1)} collective-permute-done((f32[512]{0:T(512)S(1)}, f32[512]{0:T(512)S(1)}, u32[]{:S(2)}, u32[]{:S(2)}) %collective-permute-start.13) | collective-permute-done | bytes 2080 | tf_op jit(solution)/shard_map/ppermute | solution.py:84
  153.7 0.0 collective-permute-start.14
  153.7 0.7 maximum_bitcast_fusion
  154.4 4.1 %collective-permute-done.14 = f32[512]{0:T(512)S(1)} collective-permute-done((f32[512]{0:T(512)S(1)}, f32[512]{0:T(512)S(1)}, u32[]{:S(2)}, u32[]{:S(2)}) %collective-permute-start.14) | collective-permute-done | bytes 2080 | tf_op jit(solution)/shard_map/ppermute | solution.py:84
  158.7 0.1 dynamic_slice.4
  158.8 9.2 %fusion.74 = f32[1,512]{1,0:T(1,128)S(1)} fusion(f32[4096,1]{0,1:T(1,128)S(1)} %bitcast.39, f32[512,4096]{1,0:T(8,128)} %param.15), kind=kOutput, calls=%fused_computation.186 | convolution fusion | flops 25165824 | bytes 8407040 | tf_op jit(solution)/shard_map/dot_general | solution.py:88
  168.0 0.0 copy-done.2
  168.0 0.6 add_multiply_fusion
  (38 shorter events, 0.4 us)
Async XLA Ops:
  0.6 17.0 %copy-start = (bf16[1,1,4,512,64]{3,4,2,1,0:T(8,128)(2,1)S(1)}, bf16[1,1,4,512,64]{3,4,2,1,0:T(8,128)(2,1)}, u32[]{:S(2)}) copy-start(bf16[1,1,4,512,64]{3,4,2,1,0:T(8,128)(2,1)} %param.11) | copy-start | bytes 786436
  18.0 3.5 %collective-permute-start = (f32[4,2,256]{2,1,0:T(2,128)S(1)}, f32[4,2,256]{2,1,0:T(2,128)S(1)}, u32[]{:S(2)}, u32[]{:S(2)}) collective-permute-start(f32[4,2,256]{2,1,0:T(2,128)S(1)} %get-tuple-element.55), channel_id=1, source_target_pairs={{1,0},{2,1},{3,2},{4,3},{5,4},{6,5},{7,6},{0,7},{9,8},{10,9},{11,1... | collective-permute-start | bytes 24584 | tf_op jit(solution)/shard_map/ppermute | solution.py:22
  20.1 4.9 %collective-permute-start.1 = (f32[4,2,256]{2,1,0:T(2,128)S(1)}, f32[4,2,256]{2,1,0:T(2,128)S(1)}, u32[]{:S(2)}, u32[]{:S(2)}) collective-permute-start(f32[4,2,256]{2,1,0:T(2,128)S(1)} %get-tuple-element.54), channel_id=1, source_target_pairs={{0,1},{1,2},{2,3},{3,4},{4,5},{5,6},{6,7},{7,0},{8,9},{9,10},{10,1... | collective-permute-start | bytes 24584 | tf_op jit(solution)/shard_map/ppermute | solution.py:20
  25.2 12.5 %copy-start.1 = (s32[4096]{0:T(1024)S(1)}, s32[4096]{0:T(1024)}, u32[]{:S(2)}) copy-start(s32[4096]{0:T(1024)} %param.13) | copy-start | bytes 49156
  25.2 12.5 %copy-start.4 = (u32[32]{0:T(128)S(1)}, u32[32]{0:T(128)}, u32[]{:S(2)}) copy-start(u32[32]{0:T(128)} %constant.106) | copy-start | bytes 388
  25.7 1.4 collective-permute-start.2
  25.8 4.9 %collective-permute-start.3 = (f32[4,2,256]{2,1,0:T(2,128)S(1)}, f32[4,2,256]{2,1,0:T(2,128)S(1)}, u32[]{:S(2)}, u32[]{:S(2)}) collective-permute-start(f32[4,2,256]{2,1,0:T(2,128)S(1)} %get-tuple-element.52), channel_id=1, source_target_pairs={{0,1},{1,2},{2,3},{3,4},{4,5},{5,6},{6,7},{7,0},{8,9},{9,10},{10,1... | collective-permute-start | bytes 24584 | tf_op jit(solution)/shard_map/ppermute | solution.py:20
  31.0 12.1 %copy-start.3 = (s32[1,1,4]{2,1,0:T(1,128)S(1)}, s32[1,1,4]{2,1,0:T(1,128)}, u32[]{:S(2)}) copy-start(s32[1,1,4]{2,1,0:T(1,128)} %param.10) | copy-start | bytes 52
  31.5 1.4 collective-permute-start.4
  31.5 4.9 %collective-permute-start.5 = (f32[4,2,256]{2,1,0:T(2,128)S(1)}, f32[4,2,256]{2,1,0:T(2,128)S(1)}, u32[]{:S(2)}, u32[]{:S(2)}) collective-permute-start(f32[4,2,256]{2,1,0:T(2,128)S(1)} %get-tuple-element.48), channel_id=1, source_target_pairs={{0,1},{1,2},{2,3},{3,4},{4,5},{5,6},{6,7},{7,0},{8,9},{9,10},{10,1... | collective-permute-start | bytes 24584 | tf_op jit(solution)/shard_map/ppermute | solution.py:20
  37.2 1.4 collective-permute-start.6
  37.2 4.9 %collective-permute-start.7 = (f32[4,2,256]{2,1,0:T(2,128)S(1)}, f32[4,2,256]{2,1,0:T(2,128)S(1)}, u32[]{:S(2)}, u32[]{:S(2)}) collective-permute-start(f32[4,2,256]{2,1,0:T(2,128)S(1)} %get-tuple-element.44), channel_id=1, source_target_pairs={{0,1},{1,2},{2,3},{3,4},{4,5},{5,6},{6,7},{7,0},{8,9},{9,10},{10,1... | collective-permute-start | bytes 24584 | tf_op jit(solution)/shard_map/ppermute | solution.py:20
  115.7 52.3 %copy-start.2 = (f32[512]{0:T(512)S(1)}, f32[512]{0:T(512)}, u32[]{:S(2)}) copy-start(f32[512]{0:T(512)} %param.9) | copy-start | bytes 6148
  124.9 4.8 %collective-permute-start.8 = (f32[512]{0:T(512)S(1)}, f32[512]{0:T(512)S(1)}, u32[]{:S(2)}, u32[]{:S(2)}) collective-permute-start(f32[512]{0:T(512)S(1)} %bitcast.40), channel_id=1, source_target_pairs={{0,1},{1,2},{2,3},{3,4},{4,5},{5,6},{6,7},{7,0},{8,9},{9,10},{10,1... | collective-permute-start | bytes 6152 | tf_op jit(solution)/shard_map/ppermute | solution.py:84
  129.7 4.8 %collective-permute-start.9 = (f32[512]{0:T(512)S(1)}, f32[512]{0:T(512)S(1)}, u32[]{:S(2)}, u32[]{:S(2)}) collective-permute-start(f32[512]{0:T(512)S(1)} %collective-permute-done.8), channel_id=1, source_target_pairs={{0,1},{1,2},{2,3},{3,4},{4,5},{5,6},{6,7},{7,0},{8,9},{9,10},{10,1... | collective-permute-start | bytes 6152 | tf_op jit(solution)/shard_map/ppermute | solution.py:84
  134.5 4.8 %collective-permute-start.10 = (f32[512]{0:T(512)S(1)}, f32[512]{0:T(512)S(1)}, u32[]{:S(2)}, u32[]{:S(2)}) collective-permute-start(f32[512]{0:T(512)S(1)} %collective-permute-done.9), channel_id=1, source_target_pairs={{0,1},{1,2},{2,3},{3,4},{4,5},{5,6},{6,7},{7,0},{8,9},{9,10},{10,1... | collective-permute-start | bytes 6152 | tf_op jit(solution)/shard_map/ppermute | solution.py:84
  139.3 4.8 %collective-permute-start.11 = (f32[512]{0:T(512)S(1)}, f32[512]{0:T(512)S(1)}, u32[]{:S(2)}, u32[]{:S(2)}) collective-permute-start(f32[512]{0:T(512)S(1)} %collective-permute-done.10), channel_id=1, source_target_pairs={{0,1},{1,2},{2,3},{3,4},{4,5},{5,6},{6,7},{7,0},{8,9},{9,10},{10,1... | collective-permute-start | bytes 6152 | tf_op jit(solution)/shard_map/ppermute | solution.py:84
  144.1 4.8 %collective-permute-start.12 = (f32[512]{0:T(512)S(1)}, f32[512]{0:T(512)S(1)}, u32[]{:S(2)}, u32[]{:S(2)}) collective-permute-start(f32[512]{0:T(512)S(1)} %collective-permute-done.11), channel_id=1, source_target_pairs={{0,1},{1,2},{2,3},{3,4},{4,5},{5,6},{6,7},{7,0},{8,9},{9,10},{10,1... | collective-permute-start | bytes 6152 | tf_op jit(solution)/shard_map/ppermute | solution.py:84
  148.9 4.8 %collective-permute-start.13 = (f32[512]{0:T(512)S(1)}, f32[512]{0:T(512)S(1)}, u32[]{:S(2)}, u32[]{:S(2)}) collective-permute-start(f32[512]{0:T(512)S(1)} %collective-permute-done.12), channel_id=1, source_target_pairs={{0,1},{1,2},{2,3},{3,4},{4,5},{5,6},{6,7},{7,0},{8,9},{9,10},{10,1... | collective-permute-start | bytes 6152 | tf_op jit(solution)/shard_map/ppermute | solution.py:84
  153.7 4.8 %collective-permute-start.14 = (f32[512]{0:T(512)S(1)}, f32[512]{0:T(512)S(1)}, u32[]{:S(2)}, u32[]{:S(2)}) collective-permute-start(f32[512]{0:T(512)S(1)} %collective-permute-done.13), channel_id=1, source_target_pairs={{0,1},{1,2},{2,3},{3,4},{4,5},{5,6},{6,7},{7,0},{8,9},{9,10},{10,1... | collective-permute-start | bytes 6152 | tf_op jit(solution)/shard_map/ppermute | solution.py:84
